TPU v7x, 32 devices: a whole 2x2x4 slice. The times are simulated.
32 devices in a mesh: ctx: 8 (over z, x), head: 4 (over y, core).
Axes of the slice: x: 2, y: 2, z: 4, core: 2. Of those that a mesh axis runs over, the one named last changes fastest.
Arguments:
- queries: bfloat16 [4096, 4096], P('ctx', 'head'), may hold values from -5 to 5
- keys: bfloat16 [4096, 512], P('ctx', 'head'), may hold values from -5 to 5
- values: bfloat16 [4096, 512], P('ctx', 'head'), may hold values from -8 to 8
- feature_map: bfloat16 [4, 128, 16], P('head'), may hold values from -0.5 to 0.5
- out_proj: bfloat16 [4096, 8192], P('ctx', 'head'), may hold values from -0.09375 to 0.09375
- teacher: bfloat16 [4096, 8192], P('ctx', 'head'), may hold values from -16 to 16
Outputs:
- student_out: bfloat16 [4096, 8192], P('ctx', 'head')
- loss: float32 [], replicated
- feature_grad: float32 [4, 128, 16], P('head')
All inputs are finite; a program needn't handle non-finite values.
Results may differ from a plain program's by a relative error of at most 0.006.
Values may be sent and summed in bfloat16 or wider, within the bound.
A program may use at most 128 MiB of HBM per device.

v0:
```python
import math
import jax
import jax.numpy as jnp
from jax import lax
from jax.sharding import PartitionSpec as P

D = 8192
HEAD_DIM = 128
GROUP = 8
WIN = 64
exact_mode = lax.Precision.HIGHEST


def shifted(block, axis, distance):
    devices = range(lax.axis_size(axis))
    route = [(i - distance, i) for i in devices if i - distance in devices]
    return lax.ppermute(block, axis, route)


def taylor_square(features):
    feature_count = features.shape[-1]
    outer = features[..., :, None] * features[..., None, :]
    return outer.reshape(features.shape[:-1] + (feature_count * feature_count,))


def square_grad(grad_square, features):
    feature_count = features.shape[-1]
    matrix = grad_square.reshape(features.shape + (feature_count,))
    return jnp.einsum("...fh,...h->...f", matrix, features, precision=exact_mode) + jnp.einsum(
        "...hf,...h->...f", matrix, features, precision=exact_mode
    )


def masked_total(select, member):
    shaped = select.reshape((select.shape[0],) + (1,) * (member.ndim - 1))
    return jnp.sum(jnp.where(shaped, member, jnp.zeros_like(member)), axis=0)


def window_tiles(extended, tok_rows):
    tile_count = tok_rows // WIN
    first = extended[:tok_rows].reshape((tile_count, WIN) + extended.shape[1:])
    second = extended[WIN:].reshape((tile_count, WIN) + extended.shape[1:])
    return jnp.concatenate([first, second], 1)


def local(queries, keys, values, feature_map, out_proj, teacher):
    tok_rows = queries.shape[0]
    kv_groups = keys.shape[1] // HEAD_DIM
    ctx_count = lax.axis_size("ctx")
    ctx_index = lax.axis_index("ctx")
    query_heads = queries.reshape(tok_rows, kv_groups, GROUP, HEAD_DIM)
    key_heads = keys.reshape(tok_rows, kv_groups, HEAD_DIM)
    value_float = values.reshape(tok_rows, kv_groups, HEAD_DIM).astype(jnp.float32)
    query_features = jnp.einsum(
        "tgqe,gef->tgqf", query_heads, feature_map, preferred_element_type=jnp.float32
    )
    key_features = jnp.einsum(
        "tge,gef->tgf", key_heads, feature_map, preferred_element_type=jnp.float32
    )
    rim_rows = shifted(jnp.stack([keys[tok_rows - WIN :], values[tok_rows - WIN :]]), "ctx", 1)
    keys_ext = jnp.concatenate([rim_rows[0], keys], 0).reshape(tok_rows + WIN, kv_groups, HEAD_DIM)
    values_ext = jnp.concatenate([rim_rows[1], values], 0).reshape(
        tok_rows + WIN, kv_groups, HEAD_DIM
    )
    tile_count = tok_rows // WIN
    key_tiles = window_tiles(keys_ext, tok_rows)
    value_tiles = window_tiles(values_ext, tok_rows)
    query_tiles = query_heads.reshape(tile_count, WIN, kv_groups, GROUP, HEAD_DIM)
    scores = jnp.einsum(
        "ntgqe,nsge->ngqts", query_tiles, key_tiles, preferred_element_type=jnp.float32
    ) / math.sqrt(HEAD_DIM)
    tile_pos = lax.broadcasted_iota(jnp.int32, (tile_count, WIN, 2 * WIN), 0)
    query_pos = lax.broadcasted_iota(jnp.int32, (tile_count, WIN, 2 * WIN), 1)
    key_pos = lax.broadcasted_iota(jnp.int32, (tile_count, WIN, 2 * WIN), 2)
    distance = query_pos + WIN - key_pos
    allowed = (
        (distance >= 0)
        & (distance < WIN)
        & (ctx_index * tok_rows + tile_pos * WIN + key_pos - WIN >= 0)
    )
    allowed = allowed[:, None, None]
    scores = jnp.where(allowed, scores, -jnp.inf)
    row_max = jnp.max(scores, axis=-1, keepdims=True)
    weights = jnp.where(allowed, jnp.exp(scores - row_max), 0.0)
    attn_weights = (weights / jnp.sum(weights, axis=-1, keepdims=True)).astype(jnp.bfloat16)
    window_out = jnp.einsum(
        "ngqts,nsge->ntgqe", attn_weights, value_tiles, preferred_element_type=jnp.float32
    ).reshape(tok_rows, kv_groups, GROUP, HEAD_DIM)
    causal = lax.broadcasted_iota(jnp.int32, (tok_rows, tok_rows), 0) >= lax.broadcasted_iota(
        jnp.int32, (tok_rows, tok_rows), 1
    )
    qk_inner = (
        jnp.einsum("tgqf,sgf->gqts", query_features, key_features, precision=exact_mode) / 4.0
    )
    kernel = jnp.where(causal, 1.0 + qk_inner + 0.5 * qk_inner * qk_inner, 0.0)
    numerator = jnp.einsum("gqts,sge->tgqe", kernel, value_float, precision=exact_mode)
    denominator = jnp.transpose(jnp.sum(kernel, axis=-1), (2, 0, 1))
    key_square = taylor_square(key_features)
    own_square_v = jnp.einsum("sgk,sge->gke", key_square, value_float, precision=exact_mode)
    own_linear_v = jnp.einsum("sgf,sge->gfe", key_features, value_float, precision=exact_mode)
    own_values = jnp.sum(value_float, axis=0)
    own_square_k = jnp.sum(key_square, axis=0)
    own_linear_k = jnp.sum(key_features, axis=0)
    own_count = jnp.full((kv_groups,), float(tok_rows), jnp.float32)
    gathered = (
        lax.all_gather(own_square_v[None], "ctx", axis=0, tiled=True),
        lax.all_gather(own_linear_v[None], "ctx", axis=0, tiled=True),
        lax.all_gather(own_values[None], "ctx", axis=0, tiled=True),
        lax.all_gather(own_square_k[None], "ctx", axis=0, tiled=True),
        lax.all_gather(own_linear_k[None], "ctx", axis=0, tiled=True),
        lax.all_gather(own_count[None], "ctx", axis=0, tiled=True),
    )
    lower_select = jnp.arange(ctx_count) < ctx_index
    earlier = tuple((masked_total(lower_select, member) for member in gathered))
    past_square_v, past_linear_v, past_values, past_square_k, past_linear_k, past_count = earlier
    query_square = taylor_square(query_features)
    numerator = (
        numerator
        + jnp.einsum("tgqk,gke->tgqe", query_square, past_square_v, precision=exact_mode) / 32.0
        + jnp.einsum("tgqf,gfe->tgqe", query_features, past_linear_v, precision=exact_mode) / 4.0
        + past_values[None, :, None, :]
    )
    denominator = (
        denominator
        + jnp.einsum("tgqk,gk->tgq", query_square, past_square_k, precision=exact_mode) / 32.0
        + jnp.einsum("tgqf,gf->tgq", query_features, past_linear_k, precision=exact_mode) / 4.0
        + past_count[None, :, None]
    )
    linear_out = numerator / denominator[..., None]
    head_out = (
        (linear_out + window_out)
        .astype(jnp.bfloat16)
        .reshape(tok_rows, kv_groups * GROUP * HEAD_DIM)
    )
    all_heads = lax.all_gather(head_out, "head", axis=1, tiled=True)
    proj_full = lax.all_gather(out_proj, "ctx", axis=0, tiled=True)
    projected = jnp.dot(all_heads, proj_full, preferred_element_type=jnp.float32)
    student_out = projected.astype(jnp.bfloat16)
    residual = student_out.astype(jnp.float32) - teacher.astype(jnp.float32)
    total_rows = tok_rows * ctx_count
    loss_value = lax.psum(jnp.sum(residual * residual), ("ctx", "head")) / (total_rows * D)
    d_student = (2.0 * residual / total_rows).astype(jnp.bfloat16)
    head_terms = lax.dot_general(
        d_student, proj_full, (((1,), (1,)), ((), ())), preferred_element_type=jnp.float32
    )
    head_grad = (
        lax.psum_scatter(head_terms.astype(jnp.bfloat16), "head", scatter_dimension=1, tiled=True)
        .astype(jnp.float32)
        .reshape(tok_rows, kv_groups, GROUP, HEAD_DIM)
    )
    numerator_grad = head_grad / denominator[..., None]
    denominator_grad = -jnp.sum(head_grad * linear_out, axis=-1) / denominator
    kernel_grad = (
        jnp.einsum("tgqe,sge->gqts", numerator_grad, value_float, precision=exact_mode)
        + jnp.transpose(denominator_grad, (1, 2, 0))[..., None]
    )
    inner_grad = jnp.where(causal, kernel_grad * (1.0 + qk_inner), 0.0) / 4.0
    query_grad = jnp.einsum("gqts,sgf->tgqf", inner_grad, key_features, precision=exact_mode)
    key_grad = jnp.einsum("gqts,tgqf->sgf", inner_grad, query_features, precision=exact_mode)
    query_square_grad = (
        jnp.einsum("tgqe,gke->tgqk", numerator_grad, past_square_v, precision=exact_mode)
        + denominator_grad[..., None] * past_square_k[None, :, None, :]
    ) / 32.0
    query_grad = (
        query_grad
        + (
            jnp.einsum("tgqe,gfe->tgqf", numerator_grad, past_linear_v, precision=exact_mode)
            + denominator_grad[..., None] * past_linear_k[None, :, None, :]
        )
        / 4.0
        + square_grad(query_square_grad, query_features)
    )
    own_back_square = jnp.einsum(
        "tgqk,tgqe->gke", query_square, numerator_grad, precision=exact_mode
    )
    own_back_linear = jnp.einsum(
        "tgqf,tgqe->gfe", query_features, numerator_grad, precision=exact_mode
    )
    own_den_square = jnp.einsum(
        "tgqk,tgq->gk", query_square, denominator_grad, precision=exact_mode
    )
    own_den_linear = jnp.einsum(
        "tgqf,tgq->gf", query_features, denominator_grad, precision=exact_mode
    )
    gathered_back = (
        lax.all_gather(own_back_square[None], "ctx", axis=0, tiled=True),
        lax.all_gather(own_back_linear[None], "ctx", axis=0, tiled=True),
        lax.all_gather(own_den_square[None], "ctx", axis=0, tiled=True),
        lax.all_gather(own_den_linear[None], "ctx", axis=0, tiled=True),
    )
    upper_select = jnp.arange(ctx_count) > ctx_index
    later_sums = tuple((masked_total(upper_select, member) for member in gathered_back))
    later_square, later_linear, later_den_square, later_den_linear = later_sums
    key_square_grad = (
        jnp.einsum("gke,sge->sgk", later_square, value_float, precision=exact_mode)
        + later_den_square[None]
    ) / 32.0
    key_grad = (
        key_grad
        + (
            jnp.einsum("gfe,sge->sgf", later_linear, value_float, precision=exact_mode)
            + later_den_linear[None]
        )
        / 4.0
        + square_grad(key_square_grad, key_features)
    )
    own_grad = jnp.einsum(
        "tgqe,tgqf->gef", query_heads.astype(jnp.float32), query_grad, precision=exact_mode
    ) + jnp.einsum("tge,tgf->gef", key_heads.astype(jnp.float32), key_grad, precision=exact_mode)
    feature_grad = lax.psum(own_grad, "ctx")
    return (student_out, loss_value, feature_grad)


def solution(mesh):
    return jax.shard_map(
        local,
        mesh=mesh,
        in_specs=(
            P("ctx", "head"),
            P("ctx", "head"),
            P("ctx", "head"),
            P("head", None, None),
            P("ctx", "head"),
            P("ctx", "head"),
        ),
        out_specs=(P("ctx", "head"), P(), P("head", None, None)),
        check_vma=False,
    )
```

profile of v0, /device:TPU:0, one launch (start us, length us, event | category | flops | bytes accessed | tf_op | source)
XLA Modules:
  0.0 652.8 jit_solution(9237488309166573956)
XLA Ops:
  9.4 5.4 collective-permute-start
  14.8 1.7 fusion.106
  16.7 1.9 fusion.107
  20.9 18.1 %all_gather.39 = f32[8,1,256]{2,1,0:T(1,128)S(1)} all-gather(f32[1,1,256]{2,1,0:T(1,128)S(1)} %broadcast_in_dim.148), channel_id=1, replica_groups=mesh['ctx'=8,'head'=4] {'ctx'}, dimensions={0}, use_global_device_ids=true | all-gather | bytes 9216 | tf_op jit(solution)/shard_map/all_gather | solution.py:109
  40.1 1.9 copy-done.2
  42.0 7.1 %fusion.108 = f32[1,512,8]{0,1,2:T(8,128)S(1)} fusion(f32[256,1,1]{0,1,2:T(1,128)S(1)} %bitcast.398, f32[512,8,256]{0,2,1:T(8,128)S(1)} %bitcast.367), kind=kOutput, calls=%fused_computation.168 | convolution fusion | flops 12582912 | bytes 4211712 | tf_op jit(solution)/shard_map/tgqk,gk->tgq/dot_general | solution.py:125
  49.2 1.2 copy.68
  50.4 1.3 dynamic-slice
  52.3 0.9 dynamic-update-slice
  53.9 18.1 %all-reduce.3 = (f32[128]{0:T(128)S(1)}, f32[8]{0:T(128)}) all-reduce(f32[128]{0:T(128)S(1)} %dynamic-update-slice, f32[8]{0:T(128)S(1)} %dynamic-update-slice.1), channel_id=5, replica_groups=mesh['ctx'=8,'head'=4] {'ctx'}, use_global_device_ids=true, to_apply=%add | all-reduce | flops 136 | bytes 1088
  72.8 3.4 fusion.89
  76.2 1.2 copy.69
  77.4 11.7 %fusion.7 = (f32[8,512]{1,0:T(8,128)S(1)}, f32[512,512,8]{1,0,2:T(8,128)}) fusion(pred[512,512]{0,1:T(8,128)(4,1)} %iota_compare_fusion, f32[512,8,16]{0,2,1:T(8,128)S(1)} %convolution_bitcast_fusion.2, f32[16,512]{1,0:T(8,128)} %copy-done.6), kind=kOutput, calls=%fused_computation.10 | convolution fusion | flops 417329152 | bytes 8962048 | tf_op jit(solution)/shard_map/tgqf,sgf->gqts/dot_general | solution.py:93
  89.8 31.0 %all-gather.1 = f32[128,128]{1,0:T(8,128)S(1)} all-gather(f32[16,128]{1,0:T(8,128)S(1)} %fusion.93), channel_id=3, replica_groups=mesh['ctx'=8,'head'=4] {'ctx'}, dimensions={0}, use_global_device_ids=true | all-gather | bytes 73728 | tf_op jit(solution)/shard_map/all_gather | solution.py:107
  120.9 3.2 fusion.80
  124.1 9.7 %fusion.5 = f32[8,512,128]{1,2,0:T(8,128)} fusion(f32[512,512,8]{1,0,2:T(8,128)} %get-tuple-element.13, pred[512,512]{0,1:T(8,128)(4,1)S(1)} %copy-done.17, bf16[512,128]{1,0:T(8,128)(2,1)S(1)} %copy-done.5), kind=kOutput, calls=%fused_computation.7 | convolution fusion | flops 3233808384 | bytes 10878976 | tf_op jit(solution)/shard_map/gqts,sge->tgqe/dot_general | solution.py:96
  133.9 1.3 fusion.76
  135.2 18.2 %all-gather.8 = f32[8,1,128]{2,1,0:T(1,128)S(1)} all-gather(f32[1,1,128]{2,1,0:T(1,128)S(1)} %bitcast.399), channel_id=4, replica_groups=mesh['ctx'=8,'head'=4] {'ctx'}, dimensions={0}, use_global_device_ids=true | all-gather | bytes 4608 | tf_op jit(solution)/shard_map/all_gather | solution.py:108
  155.9 1.3 fusion.27
  157.3 2.6 convolution_bitcast_fusion
  159.9 1.2 copy.52
  161.1 1.8 copy.53
  162.9 1.4 select_reduce_fusion.1
  164.3 8.5 %add_convert_fusion = (bf16[512,1,8,128]{0,3,2,1:T(8,128)(2,1)}, f32[512,1,8,128]{0,3,2,1:T(8,128)}) fusion(f32[512,1,8,128]{0,3,2,1:T(8,128)} %copy.53, f32[512,8]{0,1:T(8,128)} %bitcast.390, f32[128]{0:T(128)S(1)} %copy-done.26, f32[128,512,8]{1,0,2:T(8,128)} %fusion.80, f32[512,8,256]{0,2,1:T(8,128)} %bitcast.368, ...), kind=kOutput, calls=%fused_computation.38 | convolution fusion | flops 1614807040 | bytes 13779456 | tf_op jit(solution)/shard_map/tgqk,gke->tgqe/dot_general | solution.py:119
  173.8 30.9 %all-gather.15.cloned.1.call-done = bf16[512,4096]{0,1:T(8,128)(2,1)} async-done(((bf16[512,1024]{0,1:T(8,128)(2,1)}), bf16[512,4096]{0,1:T(8,128)(2,1)}) %all-gather.15.cloned.1.call-update) | async-done | bytes 4194320 | tf_op jit(solution)/shard_map/all_gather | solution.py:135
  204.8 229.8 %all-gather.17.cloned.1.call-done = bf16[4096,2048]{1,0:T(8,128)(2,1)} async-done(((bf16[512,2048]{1,0:T(8,128)(2,1)}), bf16[4096,2048]{1,0:T(8,128)(2,1)}) %all-gather.17.cloned.1.call-update) | async-done | bytes 16777232 | tf_op jit(solution)/shard_map/all_gather | solution.py:136
  434.6 14.8 %multiply_reduce_fusion.2 = (f32[]{:T(128)}, bf16[512,2048]{1,0:T(8,128)(2,1)S(1)}) fusion(bf16[512,2048]{1,0:T(8,128)(2,1)S(1)} %copy-done.28, bf16[512,4096]{0,1:T(8,128)(2,1)} %all-gather.15.cloned.1.call-done, bf16[4096,2048]{1,0:T(8,128)(2,1)} %all-gather.17.cloned.1.call-done), kind=kOutput, calls=%fused_computation.16 | convolution fusion | flops 8596226048 | bytes 25165828 | tf_op jit(solution)/shard_map/dot_general | solution.py:137
  449.3 1.3 copy-done.29
  450.7 13.8 %convolution_convert_fusion = bf16[512,4096]{1,0:T(8,128)(2,1)} fusion(bf16[4096,2048]{1,0:T(8,128)(2,1)} %all-gather.17.cloned.1.call-done, bf16[512,2048]{1,0:T(8,128)(2,1)S(1)} %copy-done.28, bf16[512,2048]{1,0:T(8,128)(2,1)S(1)} %get-tuple-element.21), kind=kOutput, calls=%fused_computation.9 | convolution fusion | flops 8597274624 | bytes 25165824 | tf_op jit(solution)/shard_map/dot_general | solution.py:143
  465.1 0.8 copy.98
  466.0 39.3 %psum.14 = f32[]{:T(128)} all-reduce(f32[]{:T(128)} %get-tuple-element.20), channel_id=1, replica_groups=mesh['ctx'=8,'head'=4] {'ctx','head'}, use_global_device_ids=true, to_apply=%region_13.14 | all-reduce | flops 1 | bytes 8 | tf_op jit(solution)/shard_map/psum | solution.py:141
  505.9 2.1 reduce-scatter.2.cloned.1.call-done
  508.0 1.5 copy.57
  509.5 2.3 multiply_reduce_fusion.3
  512.3 3.3 convolution_bitcast_fusion.7
  516.1 4.3 convolution_bitcast_fusion.3
  520.4 20.5 %all-gather.9 = f32[8,1,256]{2,1,0:T(1,128)S(1)} all-gather(f32[1,1,256]{2,1,0:T(1,128)S(1)} %convolution_bitcast_fusion.7), channel_id=9, replica_groups=mesh['ctx'=8,'head'=4] {'ctx'}, dimensions={0}, use_global_device_ids=true | all-gather | bytes 9216 | tf_op jit(solution)/shard_map/all_gather | solution.py:188
  540.9 1.5 convolution_bitcast_fusion.6
  542.4 30.8 %all-gather.4 = f32[128,128]{1,0:T(8,128)S(1)} all-gather(f32[16,128]{1,0:T(8,128)S(1)} %convolution_bitcast_fusion.6), channel_id=6, replica_groups=mesh['ctx'=8,'head'=4] {'ctx'}, dimensions={0}, use_global_device_ids=true | all-gather | bytes 73728 | tf_op jit(solution)/shard_map/all_gather | solution.py:187
  573.6 17.3 %all-reduce.2 = f32[128]{0:T(128)S(1)} all-reduce(f32[128]{0:T(128)S(1)} %dynamic-update-slice.2), channel_id=7, replica_groups=mesh['ctx'=8,'head'=4] {'ctx'}, use_global_device_ids=true, to_apply=%add.2 | all-reduce | flops 128 | bytes 1024
  591.7 4.1 fusion.9
  596.6 1.1 multiply_reduce_fusion.1
  597.8 2.2 fusion.38
  600.0 10.8 %fusion.3 = f32[8,512,512]{1,2,0:T(8,128)S(1)} fusion(f32[512,512,8]{1,0,2:T(8,128)S(1)} %bitcast.401, f32[8,512]{1,0:T(8,128)S(1)} %get-tuple-element.7, pred[512,512]{0,1:T(8,128)(4,1)S(1)} %copy-done.18, bf16[512,128]{1,0:T(8,128)(2,1)S(1)} %copy-done.5, f32[64,8,8,128]{3,2,1,0:T(8,128)S(1)} %bitcast.380, bf16[512,1024]{1,0:T(8,128)(2,1)S(1)} %copy-done.10), kind=kOutput, calls=%fused_computation.4 | convolution fusion | flops 3234856960 | bytes 20332544 | tf_op jit(solution)/shard_map/tgqe,sge->gqts/dot_general | solution.py:154
  610.8 4.0 fusion.31
  615.5 7.1 %convolution_bitcast_fusion.4 = f32[512,1,16]{0,2,1:T(8,128)S(1)} fusion(f32[512,8,16]{0,2,1:T(8,128)S(1)} %convolution_bitcast_fusion.2, f32[8,512,512]{1,2,0:T(8,128)S(1)} %fusion.3), kind=kOutput, calls=%fused_computation.65 | convolution fusion | flops 402653184 | bytes 8683520 | tf_op jit(solution)/shard_map/gqts,tgqf->sgf/dot_general | solution.py:159
  622.6 1.4 select_reduce_fusion
  624.9 20.0 %psum.15 = f32[1,128,16]{1,2,0:T(8,128)} all-reduce(f32[1,128,16]{1,2,0:T(8,128)S(1)} %fusion.46), channel_id=1, replica_groups=mesh['ctx'=8,'head'=4] {'ctx'}, use_global_device_ids=true, to_apply=%region_20.21 | all-reduce | flops 2048 | bytes 16384 | tf_op jit(solution)/shard_map/psum | solution.py:210
  (122 shorter events, 16.7 us)
Async XLA Ops:
  7.2 7.7 %copy-start = (bf16[1,128,16]{1,2,0:T(8,128)(2,1)S(1)}, bf16[1,128,16]{1,2,0:T(8,128)(2,1)}, u32[]{:S(2)}) copy-start(bf16[1,128,16]{1,2,0:T(8,128)(2,1)} %param.9) | copy-start | bytes 12292
  7.2 12.8 %copy-start.5 = (bf16[512,128]{1,0:T(8,128)(2,1)S(1)}, bf16[512,128]{1,0:T(8,128)(2,1)}, u32[]{:S(2)}) copy-start(bf16[512,128]{1,0:T(8,128)(2,1)} %param.8) | copy-start | bytes 393220
  7.2 31.8 %copy-start.4 = (bf16[512,1024]{1,0:T(8,128)(2,1)S(1)}, bf16[512,1024]{1,0:T(8,128)(2,1)}, u32[]{:S(2)}) copy-start(bf16[512,1024]{1,0:T(8,128)(2,1)} %param.6) | copy-start | bytes 3145732
  7.2 155.7 %all-gather.19.cloned.1.call-start = ((), (), s32[]{:S(2)}) async-start(), calls=%async_computation.4 | async-start | bytes 1179648 | tf_op jit(solution)/shard_map/all_gather | solution.py:106
  9.4 145.0 %collective-permute-start = (bf16[2,64,128]{2,1,0:T(8,128)(2,1)}, bf16[2,64,128]{2,1,0:T(8,128)(2,1)}, u32[]{:S(2)}, u32[]{:S(2)}) collective-permute-start(bf16[2,64,128]{2,1,0:T(8,128)(2,1)} %pad_maximum_fusion.2), channel_id=1, source_target_pairs={{0,4},{4,8},{8,12},{12,16},{16,20},{20,24},{24,28},{1,5},{5,9},{9,... | collective-permute-start | bytes 98312 | tf_op jit(solution)/shard_map/ppermute | solution.py:17
  16.6 4.3 copy-start.6
  18.7 186.1 %all-gather.15.cloned.1.call-start = ((), (), s32[]{:S(2)}) async-start(), calls=%async_computation.1 | async-start | bytes 5242880 | tf_op jit(solution)/shard_map/all_gather | solution.py:135
  40.0 2.0 copy-start.2
  40.1 9.0 %copy-start.21 = (f32[256]{0:T(256)}, f32[256]{0:T(256)S(1)}, u32[]{:S(2)}) copy-start(f32[256]{0:T(256)S(1)} %fusion.82) | copy-start | bytes 3076
  72.2 0.6 copy-start.23
  77.4 11.7 %copy-start.30 = (f32[8]{0:T(128)S(1)}, f32[8]{0:T(128)}, u32[]{:S(2)}) copy-start(f32[8]{0:T(128)} %get-tuple-element.4) | copy-start | bytes 100
  89.2 34.9 %copy-start.17 = (pred[512,512]{0,1:T(8,128)(4,1)S(1)}, pred[512,512]{0,1:T(8,128)(4,1)}, u32[]{:S(2)}) copy-start(pred[512,512]{0,1:T(8,128)(4,1)} %iota_compare_fusion) | copy-start | bytes 786436
  124.1 9.8 %copy-start.19 = (f32[1,512,8]{1,2,0:T(8,128)S(1)}, f32[1,512,8]{1,2,0:T(8,128)}, u32[]{:S(2)}) copy-start(f32[1,512,8]{1,2,0:T(8,128)} %copy.68) | copy-start | bytes 49156
  124.1 9.8 %copy-start.20 = (f32[1,512,8]{1,2,0:T(8,128)S(1)}, f32[1,512,8]{1,2,0:T(8,128)}, u32[]{:S(2)}) copy-start(f32[1,512,8]{1,2,0:T(8,128)} %copy.69) | copy-start | bytes 49156
  124.1 11.1 %copy-start.25 = (f32[128]{0:T(128)S(1)}, f32[128]{0:T(128)}, u32[]{:S(2)}) copy-start(f32[128]{0:T(128)} %convert_reduce_fusion) | copy-start | bytes 1540
  124.1 29.3 %copy-start.27 = (s32[64]{0:T(128)S(1)}, s32[64]{0:T(128)}, u32[]{:S(2)}) copy-start(s32[64]{0:T(128)} %iota_add_fusion) | copy-start | bytes 772
  133.9 21.3 %copy-start.8 = (bf16[512,128]{1,0:T(8,128)(2,1)S(1)}, bf16[512,128]{1,0:T(8,128)(2,1)}, u32[]{:S(2)}) copy-start(bf16[512,128]{1,0:T(8,128)(2,1)} %param.7) | copy-start | bytes 393220
  161.1 3.2 copy-start.26
  164.3 8.5 %copy-start.12 = (f32[256,128]{1,0:T(8,128)}, f32[256,128]{1,0:T(8,128)S(1)}, u32[]{:S(2)}) copy-start(f32[256,128]{1,0:T(8,128)S(1)} %select_reduce_fusion.1) | copy-start | bytes 393220
  172.8 261.8 %copy-start.28 = (bf16[512,2048]{1,0:T(8,128)(2,1)S(1)}, bf16[512,2048]{1,0:T(8,128)(2,1)}, u32[]{:S(2)}) copy-start(bf16[512,2048]{1,0:T(8,128)(2,1)} %param.11) | copy-start | bytes 6291460
  172.8 261.7 %all-gather.17.cloned.1.call-start = ((), (), s32[]{:S(2)}) async-start(), calls=%async_computation.2 | async-start | bytes 18874368 | tf_op jit(solution)/shard_map/all_gather | solution.py:136
  173.6 334.4 %reduce-scatter.2.cloned.1.call-start = ((), (), s32[]{:S(2)}) async-start(), calls=%async_computation.3 | async-start | bytes 5242880 | tf_op jit(solution)/shard_map/reduce_scatter | solution.py:147
  449.3 1.3 copy-start.29
  464.4 0.7 copy-start.14
  464.5 158.1 %all-gather.21.cloned.1.call-start = ((), (), s32[]{:S(2)}) async-start(), calls=%async_computation.5 | async-start | bytes 1179648 | tf_op jit(solution)/shard_map/all_gather | solution.py:186
  509.5 2.3 copy-start.15
  509.5 2.8 copy-start.3
  512.3 3.8 copy-start.10
  516.1 24.8 %copy-start.16 = (f32[512,1,8]{0,2,1:T(8,128)S(1)}, f32[512,1,8]{0,2,1:T(8,128)}, u32[]{:S(2)}) copy-start(f32[512,1,8]{0,2,1:T(8,128)} %fusion.76) | copy-start | bytes 49156
  540.9 50.2 %copy-start.11 = (f32[512,8]{1,0:T(8,128)S(1)}, f32[512,8]{1,0:T(8,128)}, u32[]{:S(2)}) copy-start(f32[512,8]{1,0:T(8,128)} %copy.98) | copy-start | bytes 49156
  542.4 49.3 %copy-start.13 = (f32[256,128]{1,0:T(8,128)S(1)}, f32[256,128]{1,0:T(8,128)}, u32[]{:S(2)}) copy-start(f32[256,128]{1,0:T(8,128)} %copy-done.12) | copy-start | bytes 393220
  542.4 49.3 %copy-start.22 = (f32[256]{0:T(256)S(1)}, f32[256]{0:T(256)}, u32[]{:S(2)}) copy-start(f32[256]{0:T(256)} %copy-done.21) | copy-start | bytes 3076
  595.8 4.1 slice-start
  596.6 1.1 copy-start.24
  596.6 3.4 slice-start.1
  597.8 2.2 copy-start.18
  600.0 10.8 %copy-start.7 = (f32[16,512]{1,0:T(8,128)S(1)}, f32[16,512]{1,0:T(8,128)}, u32[]{:S(2)}) copy-start(f32[16,512]{1,0:T(8,128)} %copy-done.6) | copy-start | bytes 98308
  615.5 29.4 %copy-start.1 = (bf16[1,128,16]{1,2,0:T(8,128)(2,1)S(1)}, bf16[1,128,16]{1,2,0:T(8,128)(2,1)}, u32[]{:S(2)}) copy-start(bf16[1,128,16]{1,2,0:T(8,128)(2,1)} %param.9) | copy-start | bytes 12292
  622.6 2.2 copy-start.9
Sparse Core Ops, SparseCore 0:
  18.8 40.0 all-gather.18
  173.0 31.7 all-gather.14
  206.9 227.6 all-gather.16
  464.6 43.3 reduce-scatter.1
  520.5 40.2 all-gather.20
where the time goes:
time: 660 us; the launch traced here: 653 us
  waiting for transfers between devices  264 us (40%)
  blocking collectives  213 us (32%)
  matrix products  119 us (18%)
  local copies, waits for them, and re-layouts  19.3 us (3%)
  between operations  16.9 us (3%)
  other arithmetic  14.9 us (2%)
    all_gather x1, waiting for transfers between devices, local(): proj_full = lax.all_gather(out_proj, 'ctx', axis=0, tiled=True)  230 us
    psum x1, blocking collectives, local(): lax.psum(jnp.sum(residual * residual), ('ctx', 'head')) / (total_rows * D)  39.3 us
    unnamed x2, blocking collectives  35.4 us
    all_gather x1, blocking collectives, local(): lax.all_gather(own_linear_v[None], 'ctx', axis=0, tiled=True)  31 us
    all_gather x1, waiting for transfers between devices, local(): all_heads = lax.all_gather(head_out, 'head', axis=1, tiled=True)  30.9 us
    all_gather x1, blocking collectives, local(): lax.all_gather(own_back_linear[None], 'ctx', axis=0, tiled=True)  30.8 us
    all_gather x1, blocking collectives, local(): lax.all_gather(own_den_square[None], 'ctx', axis=0, tiled=True)  20.5 us
    psum x1, blocking collectives, local(): feature_grad = lax.psum(own_grad, 'ctx')  20 us
  transfers between devices with their start and end apart: 6, of which 3 were waited for; matrix products, arithmetic and copies ran while one was open for 14% of the time, Pallas kernels for 0%

commit v1 on v0

--- a/solution.py
+++ b/solution.py
@@ -44,6 +44,27 @@
 
 
 def local(queries, keys, values, feature_map, out_proj, teacher):
+
+    def track_leaf_for(panel):
+        chip_axis = "ctx"
+        k_now = jax.lax.axis_size(chip_axis)
+        arr_next, main, local_part = (k_now, jax.lax.axis_index(chip_axis), panel.shape[0])
+        frames = [(nth, (nth + 1) % arr_next) for nth in range(arr_next)]
+        store = [(nth, (nth - 1) % arr_next) for nth in range(arr_next)]
+        y1 = jnp.zeros((*panel.shape[:0], arr_next * local_part, *panel.shape[1:]), panel.dtype)
+        y1 = lax.dynamic_update_slice_in_dim(y1, panel, main * local_part, axis=0)
+        r1 = out_arr = panel
+        val2 = arr_next // 2
+        for m in range(1, val2 + 1):
+            r1 = jax.lax.ppermute(r1, chip_axis, frames)
+            y1 = lax.dynamic_update_slice_in_dim(y1, r1, (main - m) % arr_next * local_part, axis=0)
+            if m < arr_next - val2:
+                out_arr = jax.lax.ppermute(out_arr, chip_axis, store)
+                y1 = lax.dynamic_update_slice_in_dim(
+                    y1, out_arr, (main + m) % arr_next * local_part, axis=0
+                )
+        return y1
+
     tok_rows = queries.shape[0]
     kv_groups = keys.shape[1] // HEAD_DIM
     ctx_count = lax.axis_size("ctx")
@@ -133,7 +154,7 @@
         .reshape(tok_rows, kv_groups * GROUP * HEAD_DIM)
     )
     all_heads = lax.all_gather(head_out, "head", axis=1, tiled=True)
-    proj_full = lax.all_gather(out_proj, "ctx", axis=0, tiled=True)
+    proj_full = track_leaf_for(out_proj)
     projected = jnp.dot(all_heads, proj_full, preferred_element_type=jnp.float32)
     student_out = projected.astype(jnp.bfloat16)
     residual = student_out.astype(jnp.float32) - teacher.astype(jnp.float32)

time: 660 us -> 690 us (1.045)
  waiting for transfers between devices: 264 us -> 179 us
  blocking collectives: 213 us -> 293 us
  local copies, waits for them, and re-layouts: 19.3 us -> 47.5 us
  starting transfers between devices: 5.85 us -> 17.4 us
    all_gather x1 -> x0, waiting for transfers between devices: 230 us -> none  [local(): proj_full = lax.all_gather(out_proj, 'ctx', axis=0, tiled=True)]
    ppermute x0 -> x7, waiting for transfers between devices: none -> 176 us  [the longest x3 109 us: track_leaf_for(): out_arr = jax.lax.ppermute(out_arr, chip_axis, store)]
    all_gather x1, blocking collectives: 18.1 us -> 99.7 us  [local(): lax.all_gather(own_square_k[None], 'ctx', axis=0, tiled=True)]
    all_gather x1, waiting for transfers between devices: 30.9 us -> 0.01 us  [local(): all_heads = lax.all_gather(head_out, 'head', axis=1, tiled=True)]
    dynamic_update_slice x0 -> x8, local copies, waits for them, and re-layouts: none -> 22.2 us  [the longest x4 11.2 us: track_leaf_for(): lax.dynamic_update_slice_in_dim(y1, r1, (main - m) % arr_next * local_par...]
    ppermute x0 -> x7, starting transfers between devices: none -> 15.3 us  [the longest x3 7.82 us: track_leaf_for(): out_arr = jax.lax.ppermute(out_arr, chip_axis, store)]
  transfers between devices with their start and end apart: 6 -> 12, of which waited for: 3 -> 4; matrix products, arithmetic and copies ran while one was open for 14% -> 19% of each run, Pallas kernels for 0% -> 0%
where the time goes in v1:
time: 690 us; the launch traced here: 682 us
  blocking collectives  293 us (42%)
  waiting for transfers between devices  179 us (26%)
  matrix products  113 us (16%)
  local copies, waits for them, and re-layouts  47.5 us (7%)
  starting transfers between devices  17.4 us (3%)
  between operations  16.9 us (2%)
  other arithmetic  14.8 us (2%)
    ppermute x3, waiting for transfers between devices, track_leaf_for(): out_arr = jax.lax.ppermute(out_arr, chip_axis, store)  109 us
    all_gather x1, blocking collectives, local(): lax.all_gather(own_square_k[None], 'ctx', axis=0, tiled=True)  99.7 us
    ppermute x4, waiting for transfers between devices, track_leaf_for(): r1 = jax.lax.ppermute(r1, chip_axis, frames)  67.5 us
    psum x1, blocking collectives, local(): lax.psum(jnp.sum(residual * residual), ('ctx', 'head')) / (total_rows * D)  37.7 us
    unnamed x2, blocking collectives  35.4 us
    all_gather x1, blocking collectives, local(): lax.all_gather(own_back_linear[None], 'ctx', axis=0, tiled=True)  30.8 us
    all_gather x1, blocking collectives, local(): lax.all_gather(own_linear_v[None], 'ctx', axis=0, tiled=True)  30.6 us
    all_gather x1, blocking collectives, local(): lax.all_gather(own_den_square[None], 'ctx', axis=0, tiled=True)  20.5 us
  transfers between devices with their start and end apart: 12, of which 4 were waited for; matrix products, arithmetic and copies ran while one was open for 19% of the time, Pallas kernels for 0%

profile of v1, /device:TPU:0, one launch (start us, length us, event | category | flops | bytes accessed | tf_op | source)
XLA Modules:
  0.0 681.9 jit_solution(15124361298389968121)
XLA Ops:
  7.2 3.0 collective-permute-start.1
  10.2 3.1 collective-permute-start.2
  15.4 1.9 collective-permute-start
  17.3 1.7 fusion.106
  19.2 1.9 fusion.107
  23.3 99.7 %all_gather.36 = f32[8,1,256]{2,1,0:T(1,128)S(1)} all-gather(f32[1,1,256]{2,1,0:T(1,128)S(1)} %broadcast_in_dim.151), channel_id=1, replica_groups=mesh['ctx'=8,'head'=4] {'ctx'}, dimensions={0}, use_global_device_ids=true | all-gather | bytes 9216 | tf_op jit(solution)/shard_map/all_gather | solution.py:130
  124.1 1.9 copy-done.2
  126.0 7.1 %fusion.108 = f32[1,512,8]{0,1,2:T(8,128)S(1)} fusion(f32[256,1,1]{0,1,2:T(1,128)S(1)} %bitcast.398, f32[512,8,256]{0,2,1:T(8,128)S(1)} %bitcast.367), kind=kOutput, calls=%fused_computation.176 | convolution fusion | flops 12582912 | bytes 4211712 | tf_op jit(solution)/shard_map/tgqk,gk->tgq/dot_general | solution.py:146
  137.9 18.1 %all-reduce.3 = (f32[128]{0:T(128)S(1)}, f32[8]{0:T(128)}) all-reduce(f32[128]{0:T(128)S(1)} %dynamic-update-slice, f32[8]{0:T(128)S(1)} %dynamic-update-slice.1), channel_id=5, replica_groups=mesh['ctx'=8,'head'=4] {'ctx'}, use_global_device_ids=true, to_apply=%add | all-reduce | flops 136 | bytes 1088
  156.7 3.4 fusion.89
  162.0 9.8 %fusion.7 = (f32[8,512]{1,0:T(8,128)S(1)}, f32[512,512,8]{1,0,2:T(8,128)S(1)}) fusion(pred[512,512]{0,1:T(8,128)(4,1)} %iota_compare_fusion, f32[512,8,16]{0,2,1:T(8,128)S(1)} %convolution_bitcast_fusion.2, f32[16,512]{1,0:T(8,128)} %copy-done.7), kind=kOutput, calls=%fused_computation.10 | convolution fusion | flops 417329152 | bytes 8962048 | tf_op jit(solution)/shard_map/tgqf,sgf->gqts/dot_general | solution.py:114
  171.9 30.6 %all-gather.1 = f32[128,128]{1,0:T(8,128)S(1)} all-gather(f32[16,128]{1,0:T(8,128)S(1)} %fusion.93), channel_id=3, replica_groups=mesh['ctx'=8,'head'=4] {'ctx'}, dimensions={0}, use_global_device_ids=true | all-gather | bytes 73728 | tf_op jit(solution)/shard_map/all_gather | solution.py:128
  202.6 3.2 fusion.80
  205.8 6.1 fusion.5
  213.2 18.2 %all-gather.8 = f32[8,1,128]{2,1,0:T(1,128)S(1)} all-gather(f32[1,1,128]{2,1,0:T(1,128)S(1)} %bitcast.399), channel_id=4, replica_groups=mesh['ctx'=8,'head'=4] {'ctx'}, dimensions={0}, use_global_device_ids=true | all-gather | bytes 4608 | tf_op jit(solution)/shard_map/all_gather | solution.py:129
  235.2 2.6 convolution_bitcast_fusion
  239.1 1.8 copy.53
  242.4 8.5 %add_convert_fusion = (bf16[512,1,8,128]{0,3,2,1:T(8,128)(2,1)}, f32[512,1,8,128]{0,3,2,1:T(8,128)}) fusion(f32[512,1,8,128]{0,3,2,1:T(8,128)} %copy.53, f32[512,8]{0,1:T(8,128)} %bitcast.390, f32[128]{0:T(128)S(1)} %copy-done.27, f32[128,512,8]{1,0,2:T(8,128)} %fusion.80, f32[512,8,256]{0,2,1:T(8,128)} %bitcast.368, ...), kind=kOutput, calls=%fused_computation.38 | convolution fusion | flops 1614807040 | bytes 13779456 | tf_op jit(solution)/shard_map/tgqk,gke->tgqe/dot_general | solution.py:140
  251.0 4.7 collective-permute-start.4
  255.7 67.4 %collective-permute-done.3 = bf16[512,2048]{1,0:T(8,128)(2,1)S(1)} collective-permute-done((bf16[512,2048]{1,0:T(8,128)(2,1)}, bf16[512,2048]{1,0:T(8,128)(2,1)S(1)}, u32[]{:S(2)}, u32[]{:S(2)}) %collective-permute-start.3) | collective-permute-done | bytes 2097184 | tf_op jit(solution)/shard_map/ppermute | solution.py:59
  323.1 2.4 collective-permute-start.5
  325.5 39.7 %collective-permute-done.4 = bf16[512,2048]{1,0:T(8,128)(2,1)} collective-permute-done((bf16[512,2048]{1,0:T(8,128)(2,1)}, bf16[512,2048]{1,0:T(8,128)(2,1)}, u32[]{:S(2)}, u32[]{:S(2)}) %collective-permute-start.4) | collective-permute-done | bytes 2097184 | tf_op jit(solution)/shard_map/ppermute | solution.py:62
  365.2 2.0 collective-permute-start.7
  367.3 6.2 broadcast_in_dim.157
  374.9 3.2 constant_dynamic-update-slice_fusion.6
  378.1 3.1 constant_dynamic-update-slice_fusion.5
  381.2 1.5 constant_dynamic-update-slice_fusion.4
  382.7 3.2 constant_dynamic-update-slice_fusion.3
  385.9 3.1 constant_dynamic-update-slice_fusion.2
  389.0 69.0 %collective-permute-done.6 = bf16[512,2048]{1,0:T(8,128)(2,1)} collective-permute-done((bf16[512,2048]{1,0:T(8,128)(2,1)}, bf16[512,2048]{1,0:T(8,128)(2,1)}, u32[]{:S(2)}, u32[]{:S(2)}) %collective-permute-start.6) | collective-permute-done | bytes 2097184 | tf_op jit(solution)/shard_map/ppermute | solution.py:62
  458.0 3.2 constant_dynamic-update-slice_fusion.1
  461.2 3.4 constant_dynamic-update-slice_fusion
  464.6 14.8 %multiply_reduce_fusion.2 = (f32[]{:T(128)}, bf16[512,2048]{1,0:T(8,128)(2,1)S(1)}) fusion(bf16[512,2048]{1,0:T(8,128)(2,1)S(1)} %copy-done.29, bf16[512,4096]{0,1:T(8,128)(2,1)} %all-gather.14.cloned.1.call-done, bf16[4096,2048]{1,0:T(8,128)(2,1)} %constant_dynamic-update-slice_fusion), kind=kOutput, calls=%fused_computation.16 | convolution fusion | flops 8596226048 | bytes 25165828 | tf_op jit(solution)/shard_map/dot_general | solution.py:158
  480.7 13.8 %convolution_convert_fusion = bf16[512,4096]{1,0:T(8,128)(2,1)} fusion(bf16[4096,2048]{1,0:T(8,128)(2,1)} %constant_dynamic-update-slice_fusion, bf16[512,2048]{1,0:T(8,128)(2,1)S(1)} %copy-done.29, bf16[512,2048]{1,0:T(8,128)(2,1)S(1)} %get-tuple-element.21), kind=kOutput, calls=%fused_computation.9 | convolution fusion | flops 8597274624 | bytes 25165824 | tf_op jit(solution)/shard_map/dot_general | solution.py:164
  496.0 37.7 %psum.14 = f32[]{:T(128)} all-reduce(f32[]{:T(128)} %get-tuple-element.20), channel_id=1, replica_groups=mesh['ctx'=8,'head'=4] {'ctx','head'}, use_global_device_ids=true, to_apply=%region_13.14 | all-reduce | flops 1 | bytes 8 | tf_op jit(solution)/shard_map/psum | solution.py:162
  534.4 2.7 reduce-scatter.2.cloned.1.call-done
  538.7 2.3 multiply_reduce_fusion.3
  541.5 3.3 convolution_bitcast_fusion.7
  545.2 4.3 convolution_bitcast_fusion.3
  549.5 20.5 %all-gather.9 = f32[8,1,256]{2,1,0:T(1,128)S(1)} all-gather(f32[1,1,256]{2,1,0:T(1,128)S(1)} %convolution_bitcast_fusion.7), channel_id=9, replica_groups=mesh['ctx'=8,'head'=4] {'ctx'}, dimensions={0}, use_global_device_ids=true | all-gather | bytes 9216 | tf_op jit(solution)/shard_map/all_gather | solution.py:209
  571.5 30.8 %all-gather.4 = f32[128,128]{1,0:T(8,128)S(1)} all-gather(f32[16,128]{1,0:T(8,128)S(1)} %convolution_bitcast_fusion.6), channel_id=6, replica_groups=mesh['ctx'=8,'head'=4] {'ctx'}, dimensions={0}, use_global_device_ids=true | all-gather | bytes 73728 | tf_op jit(solution)/shard_map/all_gather | solution.py:208
  602.8 17.3 %all-reduce.2 = f32[128]{0:T(128)S(1)} all-reduce(f32[128]{0:T(128)S(1)} %dynamic-update-slice.2), channel_id=7, replica_groups=mesh['ctx'=8,'head'=4] {'ctx'}, use_global_device_ids=true, to_apply=%add.2 | all-reduce | flops 128 | bytes 1024
  620.8 4.1 fusion.9
  626.9 2.2 fusion.38
  629.1 10.8 %fusion.3 = f32[8,512,512]{1,2,0:T(8,128)S(1)} fusion(f32[512,512,8]{1,0,2:T(8,128)S(1)} %bitcast.401, f32[8,512]{1,0:T(8,128)S(1)} %get-tuple-element.7, pred[512,512]{0,1:T(8,128)(4,1)S(1)} %copy-done.19, bf16[512,128]{1,0:T(8,128)(2,1)S(1)} %copy-done.5, f32[64,8,8,128]{3,2,1,0:T(8,128)S(1)} %bitcast.380, bf16[512,1024]{1,0:T(8,128)(2,1)S(1)} %copy-done.11), kind=kOutput, calls=%fused_computation.4 | convolution fusion | flops 3234856960 | bytes 20332544 | tf_op jit(solution)/shard_map/tgqe,sge->gqts/dot_general | solution.py:175
  639.9 4.0 fusion.31
  644.6 7.1 %convolution_bitcast_fusion.4 = f32[512,1,16]{0,2,1:T(8,128)S(1)} fusion(f32[512,8,16]{0,2,1:T(8,128)S(1)} %convolution_bitcast_fusion.2, f32[8,512,512]{1,2,0:T(8,128)S(1)} %fusion.3), kind=kOutput, calls=%fused_computation.65 | convolution fusion | flops 402653184 | bytes 8683520 | tf_op jit(solution)/shard_map/gqts,tgqf->sgf/dot_general | solution.py:180
  654.1 19.9 %psum.15 = f32[1,128,16]{1,2,0:T(8,128)} all-reduce(f32[1,128,16]{1,2,0:T(8,128)S(1)} %fusion.46), channel_id=1, replica_groups=mesh['ctx'=8,'head'=4] {'ctx'}, use_global_device_ids=true, to_apply=%region_20.21 | all-reduce | flops 2048 | bytes 16384 | tf_op jit(solution)/shard_map/psum | solution.py:231
  (146 shorter events, 34.6 us)
Async XLA Ops:
  7.2 10.1 %copy-start = (bf16[1,128,16]{1,2,0:T(8,128)(2,1)S(1)}, bf16[1,128,16]{1,2,0:T(8,128)(2,1)}, u32[]{:S(2)}) copy-start(bf16[1,128,16]{1,2,0:T(8,128)(2,1)} %param.9) | copy-start | bytes 12292
  7.2 15.3 %copy-start.5 = (bf16[512,128]{1,0:T(8,128)(2,1)S(1)}, bf16[512,128]{1,0:T(8,128)(2,1)}, u32[]{:S(2)}) copy-start(bf16[512,128]{1,0:T(8,128)(2,1)} %param.8) | copy-start | bytes 393220
  7.2 115.8 %copy-start.4 = (bf16[512,1024]{1,0:T(8,128)(2,1)S(1)}, bf16[512,1024]{1,0:T(8,128)(2,1)}, u32[]{:S(2)}) copy-start(bf16[512,1024]{1,0:T(8,128)(2,1)} %param.6) | copy-start | bytes 3145732
  7.2 233.7 %all-gather.16.cloned.1.call-start = ((), (), s32[]{:S(2)}) async-start(), calls=%async_computation.3 | async-start | bytes 1179648 | tf_op jit(solution)/shard_map/all_gather | solution.py:127
  7.2 235.0 %collective-permute-start.1 = (bf16[512,2048]{1,0:T(8,128)(2,1)}, bf16[512,2048]{1,0:T(8,128)(2,1)}, u32[]{:S(2)}, u32[]{:S(2)}) collective-permute-start(bf16[512,2048]{1,0:T(8,128)(2,1)} %param.10), channel_id=1, source_target_pairs={{0,4},{4,8},{8,12},{12,16},{16,20},{20,24},{24,28},{28,0},{1,5},{5... | collective-permute-start | bytes 6291464 | tf_op jit(solution)/shard_map/ppermute | solution.py:59
  10.2 240.7 %collective-permute-start.2 = (bf16[512,2048]{1,0:T(8,128)(2,1)}, bf16[512,2048]{1,0:T(8,128)(2,1)}, u32[]{:S(2)}, u32[]{:S(2)}) collective-permute-start(bf16[512,2048]{1,0:T(8,128)(2,1)} %param.10), channel_id=1, source_target_pairs={{0,28},{4,0},{8,4},{12,8},{16,12},{20,16},{24,20},{28,24},{1,29},{... | collective-permute-start | bytes 6291464 | tf_op jit(solution)/shard_map/ppermute | solution.py:62
  15.4 216.9 %collective-permute-start = (bf16[2,64,128]{2,1,0:T(8,128)(2,1)}, bf16[2,64,128]{2,1,0:T(8,128)(2,1)}, u32[]{:S(2)}, u32[]{:S(2)}) collective-permute-start(bf16[2,64,128]{2,1,0:T(8,128)(2,1)} %pad_maximum_fusion.2), channel_id=1, source_target_pairs={{0,4},{4,8},{8,12},{12,16},{16,20},{20,24},{24,28},{1,5},{5,9},{9,... | collective-permute-start | bytes 98312 | tf_op jit(solution)/shard_map/ppermute | solution.py:17
  19.0 4.3 copy-start.7
  21.1 443.5 %all-gather.14.cloned.1.call-start = ((), (), s32[]{:S(2)}) async-start(), calls=%async_computation.1 | async-start | bytes 5242880 | tf_op jit(solution)/shard_map/all_gather | solution.py:156
  124.0 2.0 copy-start.2
  124.1 9.0 %copy-start.22 = (f32[256]{0:T(256)}, f32[256]{0:T(256)S(1)}, u32[]{:S(2)}) copy-start(f32[256]{0:T(256)S(1)} %fusion.82) | copy-start | bytes 3076
  156.2 0.5 copy-start.24
  156.7 4.7 copy-start.31
  171.9 40.0 %copy-start.32 = (f32[512,512,8]{1,0,2:T(8,128)}, f32[512,512,8]{1,0,2:T(8,128)S(1)}, u32[]{:S(2)}) copy-start(f32[512,512,8]{1,0,2:T(8,128)S(1)} %get-tuple-element.13) | copy-start | bytes 25165828
  171.9 33.9 %copy-start.18 = (pred[512,512]{0,1:T(8,128)(4,1)S(1)}, pred[512,512]{0,1:T(8,128)(4,1)}, u32[]{:S(2)}) copy-start(pred[512,512]{0,1:T(8,128)(4,1)} %iota_compare_fusion) | copy-start | bytes 786436
  205.8 6.1 copy-start.20
  205.8 6.1 copy-start.21
  205.8 7.4 %copy-start.26 = (f32[128]{0:T(128)S(1)}, f32[128]{0:T(128)}, u32[]{:S(2)}) copy-start(f32[128]{0:T(128)} %convert_reduce_fusion) | copy-start | bytes 1540
  205.8 25.5 %copy-start.28 = (s32[64]{0:T(128)S(1)}, s32[64]{0:T(128)}, u32[]{:S(2)}) copy-start(s32[64]{0:T(128)} %iota_add_fusion) | copy-start | bytes 772
  211.9 21.2 %copy-start.9 = (bf16[512,128]{1,0:T(8,128)(2,1)S(1)}, bf16[512,128]{1,0:T(8,128)(2,1)}, u32[]{:S(2)}) copy-start(bf16[512,128]{1,0:T(8,128)(2,1)} %param.7) | copy-start | bytes 393220
  239.0 3.4 copy-start.27
  242.3 8.6 %copy-start.13 = (f32[256,128]{1,0:T(8,128)}, f32[256,128]{1,0:T(8,128)S(1)}, u32[]{:S(2)}) copy-start(f32[256,128]{1,0:T(8,128)S(1)} %select_reduce_fusion.1) | copy-start | bytes 393220
  242.3 80.9 %collective-permute-start.3 = (bf16[512,2048]{1,0:T(8,128)(2,1)}, bf16[512,2048]{1,0:T(8,128)(2,1)S(1)}, u32[]{:S(2)}, u32[]{:S(2)}) collective-permute-start(bf16[512,2048]{1,0:T(8,128)(2,1)} %collective-permute-done.1), channel_id=1, source_target_pairs={{0,4},{4,8},{8,12},{12,16},{16,20},{20,24},{24,28},{28,0},{1,5},{5... | collective-permute-start | bytes 6291464 | tf_op jit(solution)/shard_map/ppermute | solution.py:59
  250.9 286.2 %reduce-scatter.2.cloned.1.call-start = ((), (), s32[]{:S(2)}) async-start(), calls=%async_computation.2 | async-start | bytes 5242880 | tf_op jit(solution)/shard_map/reduce_scatter | solution.py:168
  251.0 114.2 %collective-permute-start.4 = (bf16[512,2048]{1,0:T(8,128)(2,1)}, bf16[512,2048]{1,0:T(8,128)(2,1)}, u32[]{:S(2)}, u32[]{:S(2)}) collective-permute-start(bf16[512,2048]{1,0:T(8,128)(2,1)} %collective-permute-done.2), channel_id=1, source_target_pairs={{0,28},{4,0},{8,4},{12,8},{16,12},{20,16},{24,20},{28,24},{1,29},{... | collective-permute-start | bytes 6291464 | tf_op jit(solution)/shard_map/ppermute | solution.py:62
  323.1 42.1 %collective-permute-start.5 = (bf16[512,2048]{1,0:T(8,128)(2,1)S(1)}, bf16[512,2048]{1,0:T(8,128)(2,1)}, u32[]{:S(2)}, u32[]{:S(2)}) collective-permute-start(bf16[512,2048]{1,0:T(8,128)(2,1)S(1)} %collective-permute-done.3), channel_id=1, source_target_pairs={{0,4},{4,8},{8,12},{12,16},{16,20},{20,24},{24,28},{28,0},{1,5},{5... | collective-permute-start | bytes 6291464 | tf_op jit(solution)/shard_map/ppermute | solution.py:59
  365.2 92.8 %collective-permute-start.6 = (bf16[512,2048]{1,0:T(8,128)(2,1)}, bf16[512,2048]{1,0:T(8,128)(2,1)}, u32[]{:S(2)}, u32[]{:S(2)}) collective-permute-start(bf16[512,2048]{1,0:T(8,128)(2,1)} %collective-permute-done.4), channel_id=1, source_target_pairs={{0,28},{4,0},{8,4},{12,8},{16,12},{20,16},{24,20},{28,24},{1,29},{... | collective-permute-start | bytes 6291464 | tf_op jit(solution)/shard_map/ppermute | solution.py:62
  365.2 96.0 %collective-permute-start.7 = (bf16[512,2048]{1,0:T(8,128)(2,1)}, bf16[512,2048]{1,0:T(8,128)(2,1)}, u32[]{:S(2)}, u32[]{:S(2)}) collective-permute-start(bf16[512,2048]{1,0:T(8,128)(2,1)} %collective-permute-done.5), channel_id=1, source_target_pairs={{0,4},{4,8},{8,12},{12,16},{16,20},{20,24},{24,28},{28,0},{1,5},{5... | collective-permute-start | bytes 6291464 | tf_op jit(solution)/shard_map/ppermute | solution.py:59
  367.3 6.2 copy-start.6
  461.2 3.4 copy-start.29
  479.4 1.3 copy-start.30
  494.5 0.7 copy-start.15
  494.5 157.2 %all-gather.18.cloned.1.call-start = ((), (), s32[]{:S(2)}) async-start(), calls=%async_computation.4 | async-start | bytes 1179648 | tf_op jit(solution)/shard_map/all_gather | solution.py:207
  538.7 2.3 copy-start.16
  538.7 2.8 copy-start.3
  541.5 3.8 copy-start.11
  545.2 24.8 %copy-start.17 = (f32[512,1,8]{0,2,1:T(8,128)S(1)}, f32[512,1,8]{0,2,1:T(8,128)}, u32[]{:S(2)}) copy-start(f32[512,1,8]{0,2,1:T(8,128)} %fusion.76) | copy-start | bytes 49156
  570.0 50.2 %copy-start.12 = (f32[512,8]{1,0:T(8,128)S(1)}, f32[512,8]{1,0:T(8,128)}, u32[]{:S(2)}) copy-start(f32[512,8]{1,0:T(8,128)} %copy.98) | copy-start | bytes 49156
  571.5 49.3 %copy-start.14 = (f32[256,128]{1,0:T(8,128)S(1)}, f32[256,128]{1,0:T(8,128)}, u32[]{:S(2)}) copy-start(f32[256,128]{1,0:T(8,128)} %copy-done.13) | copy-start | bytes 393220
  571.5 49.3 %copy-start.23 = (f32[256]{0:T(256)S(1)}, f32[256]{0:T(256)}, u32[]{:S(2)}) copy-start(f32[256]{0:T(256)} %copy-done.22) | copy-start | bytes 3076
  625.0 4.1 slice-start
  625.7 1.1 copy-start.25
  625.8 3.4 slice-start.1
  626.9 2.2 copy-start.19
  629.1 10.8 %copy-start.8 = (f32[16,512]{1,0:T(8,128)S(1)}, f32[16,512]{1,0:T(8,128)}, u32[]{:S(2)}) copy-start(f32[16,512]{1,0:T(8,128)} %copy-done.7) | copy-start | bytes 98308
  644.6 29.4 %copy-start.1 = (bf16[1,128,16]{1,2,0:T(8,128)(2,1)S(1)}, bf16[1,128,16]{1,2,0:T(8,128)(2,1)}, u32[]{:S(2)}) copy-start(bf16[1,128,16]{1,2,0:T(8,128)(2,1)} %param.9) | copy-start | bytes 12292
  651.7 2.2 copy-start.10
Sparse Core Ops, SparseCore 0:
  21.2 74.2 all-gather.15
  251.1 35.8 all-gather.13
  494.6 42.4 reduce-scatter.1
  549.6 40.2 all-gather.17
